TPU v7x, 32 devices: a whole 2x2x4 slice. The times are simulated.
32 devices in a mesh: req: 8 (over z, x), head: 4 (over y, core).
Axes of the slice: x: 2, y: 2, z: 4, core: 2. Of those that a mesh axis runs over, the one named last changes fastest.
Arguments:
- residual_in: bfloat16 [1024, 1536], P(('req', 'head')), may hold values from -3 to 3
- attn_gain: bfloat16 [1536], replicated, may hold values from 0.099609375 to 1.8984375
- w_qkv: bfloat16 [1536, 8, 320], P(None, 'head'), may hold values from -0.15625 to 0.15625
- w_out: bfloat16 [1536, 1536], P('head'), may hold values from -0.41992188 to 0.41992188
- kv_cache: bfloat16 [1024, 8, 192, 128], P('req', 'head'), as said below
- lengths: int32 [1024], P('req'), may hold values from 1 to 192, as said below
- moe_gain: bfloat16 [1536], replicated, may hold values from 0.099609375 to 1.8984375
- w_router: bfloat16 [1536, 24], replicated
- routes: int32 [1024, 8], P(('req', 'head')), may hold values from 0 to 23, all different within a row; in each aligned block of 32 rows (0 to 31, 32 to 63, ...) at most 12 rows name the same one
- w_in: bfloat16 [24, 1536, 1024], P('req'), may hold values from -0.15625 to 0.15625
- w_down: bfloat16 [24, 512, 1536], P('req'), may hold values from -0.5 to 0.5
Outputs:
- layer_out: bfloat16 [1024, 1536], P(('req', 'head'))
- new_kv: bfloat16 [1024, 8, 128], P('req', 'head')
Inputs may be any that keep to these rules, and one draw needn't show every extreme that they name: `kv_cache`: each position holds its key in the first 64 entries and its value in the last 64. `lengths`: some request has exactly 192 cached positions. `routes`: each row names 8 different experts. Among the 32 rows of one device no expert is named more than 12 times, a bound that some block reaches.
All inputs are finite; a program needn't handle non-finite values.
Results may differ from a plain program's by a relative error of at most 0.017.
Values may be sent and summed in bfloat16 or wider, within the bound.
A program may use at most 128 MiB of HBM per device.

v0:
```python
import jax
import jax.numpy as jnp
from jax import lax
from jax.sharding import PartitionSpec as P

D = 1536
HEADS = 24
KV = 8
HD = 64
F = 512
EPSILON = 1e-06
THETA = 10000.0


def rms_scale(values, gain):
    wide = values.astype(jnp.float32)
    mean_square = jnp.mean(wide * wide, axis=-1, keepdims=True)
    return (wide * lax.rsqrt(mean_square + EPSILON) * gain.astype(jnp.float32)).astype(jnp.bfloat16)


def rotate(vectors, lengths):
    half = vectors.shape[-1] // 2
    index = jnp.arange(half).astype(jnp.float32)
    frequency = jnp.power(THETA, -2.0 * index / vectors.shape[-1])
    angle = lengths.astype(jnp.float32)[:, None] * frequency[None, :]
    cosine = jnp.cos(angle)[:, None, None, :]
    sine = jnp.sin(angle)[:, None, None, :]
    first = vectors[..., :half]
    second = vectors[..., half:]
    return jnp.concatenate(
        [first * cosine - second * sine, second * cosine + first * sine], axis=-1
    )


def project_heads(projected, lengths, group, head_size):
    blocks = projected.reshape(projected.shape[0], -1, group + 2, head_size)
    queries = rotate(blocks[:, :, :group], lengths).astype(jnp.bfloat16)
    new_keys = rotate(blocks[:, :, group : group + 1], lengths).astype(jnp.bfloat16)[:, :, 0]
    new_values = blocks[:, :, group + 1].astype(jnp.bfloat16)
    return (queries, new_keys, new_values)


def own_scores(queries, new_keys):
    product = queries.astype(jnp.float32) * new_keys.astype(jnp.float32)[:, :, None, :]
    return jnp.sum(product, axis=-1) * HD ** (-0.5)


def own_term(own_weight, new_values):
    own_prob = own_weight.astype(jnp.bfloat16).astype(jnp.float32)
    return own_prob[..., None] * new_values.astype(jnp.float32)[:, :, None, :]


def attend_full(queries, new_keys, new_values, cache, lengths):
    scores = jnp.einsum(
        "rkgd,rkld->rkgl", queries, cache[..., :HD], preferred_element_type=jnp.float32
    ) * HD ** (-0.5)
    own = own_scores(queries, new_keys)
    positions = jnp.arange(cache.shape[2])
    live = (positions[None, :] < lengths[:, None])[:, None, None, :]
    masked = jnp.where(live, scores, -1e30)
    peak = jnp.maximum(jnp.max(masked, axis=-1), own)
    weights = jnp.where(live, jnp.exp(masked - peak[..., None]), 0.0)
    own_weight = jnp.exp(own - peak)
    total = jnp.sum(weights, axis=-1) + own_weight
    probabilities = weights.astype(jnp.bfloat16)
    weighted = jnp.einsum(
        "rkgl,rkld->rkgd", probabilities, cache[..., HD:], preferred_element_type=jnp.float32
    )
    weighted = weighted + own_term(own_weight, new_values)
    return (weighted / total[..., None]).astype(jnp.bfloat16)


def local(
    residual_in,
    attn_gain,
    w_qkv,
    w_out,
    kv_cache,
    lengths,
    moe_gain,
    w_router,
    routes,
    w_in,
    w_down,
):
    group = HEADS // KV
    tok_rows = residual_in.shape[0]
    req_rows = lengths.shape[0]
    kv_local = w_qkv.shape[1]
    normed = rms_scale(residual_in, attn_gain)
    flat_weight = w_qkv.reshape(D, kv_local * (group + 2) * HD)
    projected = jnp.dot(
        lax.all_gather(normed, "head", axis=0, tiled=True),
        flat_weight,
        preferred_element_type=jnp.float32,
    )
    queries, new_keys, new_values = project_heads(projected, lengths, group, HD)
    new_kv = jnp.concatenate([new_keys, new_values], axis=-1)
    heads_out = attend_full(queries, new_keys, new_values, kv_cache, lengths)
    local_width = kv_local * group * HD
    attn_heads = heads_out.reshape(req_rows, local_width)
    attention = lax.psum_scatter(
        jnp.dot(attn_heads, w_out, preferred_element_type=jnp.float32).astype(jnp.bfloat16),
        "head",
        scatter_dimension=0,
        tiled=True,
    ).astype(jnp.float32)
    attended = (residual_in.astype(jnp.float32) + attention).astype(jnp.bfloat16)
    normed_moe = rms_scale(attended, moe_gain)
    logits = jnp.dot(normed_moe, w_router, preferred_element_type=jnp.float32)
    gates = jax.nn.softmax(jnp.take_along_axis(logits, routes, axis=1), axis=-1)
    top = routes.shape[1]
    experts_all = w_router.shape[1]
    owners = lax.axis_size("req")
    local_experts = w_in.shape[0]
    capacity = (tok_rows * top + experts_all - 1) // experts_all + 1
    chosen = routes.reshape(tok_rows * top)
    onehot = (chosen[:, None] == jnp.arange(experts_all)[None, :]).astype(jnp.int32)
    earlier = jnp.cumsum(onehot, axis=0) - onehot
    within = jnp.sum(earlier * onehot, axis=1)
    slots = chosen * capacity + within
    placed = (slots[:, None] == jnp.arange(experts_all * capacity)[None, :]).astype(jnp.bfloat16)
    source = jnp.repeat(normed_moe, top, axis=0)
    outgoing = jnp.einsum("ps,pd->sd", placed, source, preferred_element_type=jnp.float32).astype(
        jnp.bfloat16
    )
    outgoing = outgoing.reshape(owners, local_experts, capacity, D)
    both = jnp.einsum(
        "sjcd,jdf->sjcf",
        lax.all_to_all(outgoing, "req", split_axis=0, concat_axis=0, tiled=True),
        w_in,
        preferred_element_type=jnp.float32,
    )
    hidden = (jax.nn.silu(both[..., :F]) * both[..., F:]).astype(jnp.bfloat16)
    result = jnp.einsum(
        "sjcf,jfd->sjcd", hidden, w_down, preferred_element_type=jnp.float32
    ).astype(jnp.bfloat16)
    returned = lax.all_to_all(result, "req", split_axis=0, concat_axis=0, tiled=True)
    picked = jnp.take(returned.reshape(experts_all * capacity, D), slots, axis=0).reshape(
        tok_rows, top, D
    )
    mixed = jnp.sum(gates[:, :, None] * picked.astype(jnp.float32), axis=1)
    layer_out = (attended.astype(jnp.float32) + mixed).astype(jnp.bfloat16)
    return (layer_out, new_kv)


def solution(mesh):
    return jax.shard_map(
        local,
        mesh=mesh,
        in_specs=(
            P(("req", "head"), None),
            P(),
            P(None, "head", None),
            P("head", None),
            P("req", "head", None, None),
            P("req"),
            P(),
            P(),
            P(("req", "head"), None),
            P("req", None, None),
            P("req", None, None),
        ),
        out_specs=(P(("req", "head"), None), P("req", "head", None)),
        check_vma=False,
    )
```

profile of v0, /device:TPU:0, one launch (start us, length us, event | category | flops | bytes accessed | tf_op | source)
XLA Modules:
  0.0 164.2 jit_solution(350964640558112470)
XLA Ops:
  7.2 0.8 convert_element_type.116
  8.0 0.7 iota_compare_fusion.2
  8.8 1.0 fusion.46
  9.8 0.7 convert_element_type.114
  10.5 1.0 fusion.48
  11.5 7.9 %all_gather.3 = bf16[128,1536]{1,0:T(8,128)(2,1)S(1)} all-gather(bf16[32,1536]{1,0:T(8,128)(2,1)S(1)} %fusion.48), channel_id=1, replica_groups=mesh['req'=8,'head'=4] {'head'}, dimensions={0}, use_global_device_ids=true | all-gather | bytes 491520 | tf_op jit(solution)/shard_map/all_gather | solution.py:93
  20.4 0.8 copy.89
  21.3 12.0 %fusion.69 = (f32[128,2,3]{2,1,0:T(2,128)}, f32[128,2,3,192]{3,2,1,0:T(4,128)S(1)}) fusion(bf16[128,2,3,64]{3,2,1,0:T(4,128)(2,1)S(1)} %copy.81, bf16[128,2,192,128]{3,2,1,0:T(8,128)(2,1)} %param.15, pred[128,192]{1,0:T(8,128)(4,1)S(1)} %iota_compare_fusion.2), kind=kOutput, calls=%fused_computation.101 | convolution fusion | flops 19315968 | bytes 13298688 | tf_op jit(solution)/shard_map/rkgd,rkld->rkgl/dot_general | solution.py:54
  33.3 1.1 copy.85
  34.6 0.8 fusion.35
  35.6 0.8 copy.88
  36.4 0.8 copy.91
  37.2 9.9 %fusion.30 = bf16[128,2,3,64]{3,2,1,0:T(4,128)(2,1)} fusion(bf16[128,2,192,128]{3,2,1,0:T(8,128)(2,1)} %param.15, f32[128,2,3,192]{3,2,1,0:T(4,128)} %copy-done.3, f32[128,2,3]{2,1,0:T(2,128)S(1)} %copy.86, pred[128,192]{1,0:T(8,128)(4,1)S(1)} %iota_compare_fusion.2, f32[128,2,3]{2,1,0:T(2,128)} %copy.91, f32[128,2,64]{2,1,0:T(2,128)} %copy.89, ...), kind=kOutput, calls=%fused_computation.22 | convolution fusion | flops 19513344 | bytes 13370368 | tf_op jit(solution)/shard_map/rkgl,rkld->rkgd/dot_general | solution.py:66
  47.1 1.1 copy.92
  48.2 1.1 convolution_convert_fusion.1
  50.6 20.7 %reduce-scatter.2.cloned.1.call-done = bf16[32,1536]{1,0:T(8,128)(2,1)} async-done(((bf16[128,1536]{1,0:T(8,128)(2,1)}), bf16[32,1536]{1,0:T(8,128)(2,1)}) %reduce-scatter.2.cloned.1.call-update) | async-done | bytes 98320 | tf_op jit(solution)/shard_map/reduce_scatter | solution.py:102
  71.3 1.0 fusion.50
  72.3 1.0 fusion.52
  73.9 1.2 reshape.241
  75.1 5.5 %all-to-all-start = ((bf16[8,3,12,1536]{3,2,1,0:T(8,128)(2,1)}), bf16[8,3,12,1536]{3,2,1,0:T(8,128)(2,1)S(1)}, u32[]{:S(2)}, u32[]{:S(2)}) async-start(bf16[8,3,12,1536]{3,2,1,0:T(8,128)(2,1)} %reshape.241), calls=%async_computation.1 | async-start | bytes 2359296 | tf_op jit(solution)/shard_map/all_to_all | solution.py:130
  80.8 28.4 %all-to-all-done = bf16[8,3,12,1536]{3,2,1,0:T(8,128)(2,1)S(1)} async-done(((bf16[8,3,12,1536]{3,2,1,0:T(8,128)(2,1)}), bf16[8,3,12,1536]{3,2,1,0:T(8,128)(2,1)S(1)}, u32[]{:S(2)}, u32[]{:S(2)}) %all-to-all-start) | async-done | bytes 884768 | tf_op jit(solution)/shard_map/all_to_all | solution.py:130
  109.1 5.1 %fusion.14 = f32[8,3,12,1024]{3,2,0,1:T(8,128)S(1)} fusion(bf16[3,1536,1024]{2,1,0:T(8,128)(2,1)} %param.20, bf16[8,3,12,1536]{3,2,1,0:T(8,128)(2,1)S(1)} %all-to-all-done), kind=kOutput, calls=%fused_computation.15 | convolution fusion | flops 905969664 | bytes 11501568 | tf_op jit(solution)/shard_map/sjcd,jdf->sjcf/dot_general | solution.py:128
  114.2 3.2 %fusion.11 = bf16[8,3,12,1536]{3,2,0,1:T(8,128)(2,1)S(1)} fusion(bf16[3,512,1536]{2,1,0:T(8,128)(2,1)} %param.21, f32[8,3,12,1024]{3,2,0,1:T(8,128)S(1)} %fusion.14), kind=kOutput, calls=%fused_computation.12 | convolution fusion | flops 454311936 | bytes 6782976 | tf_op jit(solution)/shard_map/sjcf,jfd->sjcd/dot_general | solution.py:135
  117.5 1.1 copy.101
  118.6 4.2 %all-to-all-start.1 = ((bf16[8,3,12,1536]{3,2,1,0:T(8,128)(2,1)}), bf16[8,3,12,1536]{3,2,1,0:T(8,128)(2,1)}, u32[]{:S(2)}, u32[]{:S(2)}) async-start(bf16[8,3,12,1536]{3,2,1,0:T(8,128)(2,1)} %copy.101), calls=%async_computation.2 | async-start | bytes 2359296 | tf_op jit(solution)/shard_map/all_to_all | solution.py:138
  123.0 0.8 copy.102
  123.9 2.0 %gather_fusion.1 = f32[256]{0:T(256)S(1)} fusion(f32[32,24]{0,1:T(8,128)S(1)} %fusion.70, s32[256]{0:T(256)S(1)} %reshape.251), kind=kCustom, calls=%fused_computation.1 | custom fusion | bytes 4096 | tf_op jit(solution)/shard_map/jit(take_along_axis)/gather | solution.py:111
  126.4 24.8 %all-to-all-done.1 = bf16[8,3,12,1536]{3,2,1,0:T(8,128)(2,1)} async-done(((bf16[8,3,12,1536]{3,2,1,0:T(8,128)(2,1)}), bf16[8,3,12,1536]{3,2,1,0:T(8,128)(2,1)}, u32[]{:S(2)}, u32[]{:S(2)}) %all-to-all-start.1) | async-done | bytes 884768 | tf_op jit(solution)/shard_map/all_to_all | solution.py:138
  151.2 1.3 reshape.242
  152.5 2.1 %gather_fusion = bf16[256,1536]{1,0:T(8,128)(2,1)} fusion(bf16[288,1536]{1,0:T(8,128)(2,1)S(1)} %reshape.242, s32[1024]{0:T(1024)S(1)} %pad_clamp_fusion), kind=kCustom, calls=%fused_computation | custom fusion | bytes 1573888 | tf_op jit(solution)/shard_map/jit(_take)/gather | solution.py:139
  154.7 2.0 %multiply_reduce_fusion = f32[32,1536]{1,0:T(8,128)S(1)} fusion(bf16[256,1536]{1,0:T(8,128)(2,1)} %gather_fusion, f32[32,8]{1,0:T(8,128)S(1)} %fusion.62, pred[32,8]{1,0:T(8,128)(4,1)S(1)} %compare_and_fusion), kind=kLoop, calls=%fused_computation.14 | loop fusion | flops 1523712 | bytes 984320 | tf_op jit(solution)/shard_map/reduce_sum | solution.py:142
  156.7 0.7 fusion.53
  (60 shorter events, 4.1 us)
Async XLA Ops:
  7.2 12.3 %copy-start = (bf16[1536,2,320]{0,2,1:T(8,128)(2,1)S(1)}, bf16[1536,2,320]{0,2,1:T(8,128)(2,1)}, u32[]{:S(2)}) copy-start(bf16[1536,2,320]{0,2,1:T(8,128)(2,1)} %param.13) | copy-start | bytes 5898244
  7.2 64.1 %reduce-scatter.2.cloned.1.call-start = ((), (), s32[]{:S(2)}) async-start(), calls=%async_computation.3 | async-start | bytes 491520 | tf_op jit(solution)/shard_map/reduce_scatter | solution.py:102
  33.3 3.0 %copy-start.3 = (f32[128,2,3,192]{3,2,1,0:T(4,128)}, f32[128,2,3,192]{3,2,1,0:T(4,128)S(1)}, u32[]{:S(2)}) copy-start(f32[128,2,3,192]{3,2,1,0:T(4,128)S(1)} %get-tuple-element.21) | copy-start | bytes 1769476
  37.2 11.1 %copy-start.2 = (bf16[384,1536]{1,0:T(8,128)(2,1)S(1)}, bf16[384,1536]{1,0:T(8,128)(2,1)}, u32[]{:S(2)}) copy-start(bf16[384,1536]{1,0:T(8,128)(2,1)} %param.14) | copy-start | bytes 3538948
  47.1 2.3 %copy-start.6 = (s32[32,8]{0,1:T(8,128)S(1)}, s32[32,8]{0,1:T(8,128)}, u32[]{:S(2)}) copy-start(s32[32,8]{0,1:T(8,128)} %param.19) | copy-start | bytes 3076
  47.1 2.6 %copy-start.7 = (bf16[1536]{0:T(1024)(128)(2,1)S(1)}, bf16[1536]{0:T(1024)(128)(2,1)}, u32[]{:S(2)}) copy-start(bf16[1536]{0:T(1024)(128)(2,1)} %param.17) | copy-start | bytes 9220
  47.1 24.2 %copy-start.1 = (bf16[32,1536]{1,0:T(8,128)(2,1)S(1)}, bf16[32,1536]{1,0:T(8,128)(2,1)}, u32[]{:S(2)}) copy-start(bf16[32,1536]{1,0:T(8,128)(2,1)} %param.11) | copy-start | bytes 294916
  75.1 34.1 %all-to-all-start = ((bf16[8,3,12,1536]{3,2,1,0:T(8,128)(2,1)}), bf16[8,3,12,1536]{3,2,1,0:T(8,128)(2,1)S(1)}, u32[]{:S(2)}, u32[]{:S(2)}) async-start(bf16[8,3,12,1536]{3,2,1,0:T(8,128)(2,1)} %reshape.241), calls=%async_computation.1 | async-start | bytes 2359296 | tf_op jit(solution)/shard_map/all_to_all | solution.py:130
  117.4 6.3 %copy-start.5 = (bf16[1536,24]{0,1:T(8,128)(2,1)S(1)}, bf16[1536,24]{0,1:T(8,128)(2,1)}, u32[]{:S(2)}) copy-start(bf16[1536,24]{0,1:T(8,128)(2,1)} %param.18) | copy-start | bytes 221188
  118.6 32.6 %all-to-all-start.1 = ((bf16[8,3,12,1536]{3,2,1,0:T(8,128)(2,1)}), bf16[8,3,12,1536]{3,2,1,0:T(8,128)(2,1)}, u32[]{:S(2)}, u32[]{:S(2)}) async-start(bf16[8,3,12,1536]{3,2,1,0:T(8,128)(2,1)} %copy.101), calls=%async_computation.2 | async-start | bytes 2359296 | tf_op jit(solution)/shard_map/all_to_all | solution.py:138
  152.5 4.1 %copy-start.4 = (bf16[32,1536]{1,0:T(8,128)(2,1)S(1)}, bf16[32,1536]{1,0:T(8,128)(2,1)}, u32[]{:S(2)}) copy-start(bf16[32,1536]{1,0:T(8,128)(2,1)} %reduce-scatter.2.cloned.1.call-done) | copy-start | bytes 294916
Sparse Core Ops, SparseCore 0:
  49.5 21.7 reduce-scatter.1
where the time goes:
time: 165 us; the launch traced here: 164 us
  waiting for transfers between devices  73.8 us (45%)
  matrix products  32.6 us (20%)
  local copies, waits for them, and re-layouts  14.4 us (9%)
  between operations  14.3 us (9%)
  other arithmetic  11.2 us (7%)
  starting transfers between devices  9.81 us (6%)
  blocking collectives  7.94 us (5%)
    all_to_all x1, waiting for transfers between devices, local(): lax.all_to_all(outgoing, 'req', split_axis=0, concat_axis=0, tiled=True)  28.4 us
    all_to_all x1, waiting for transfers between devices, local(): lax.all_to_all(result, 'req', split_axis=0, concat_axis=0, tiled=True)  24.8 us
    reduce_scatter x1, waiting for transfers between devices, local(): lax.psum_scatter(jnp.dot(attn_heads, w_out, preferred_element_type=jnp.fl...  20.7 us
    dot_general x1, matrix products, attend_full(): jnp.einsum('rkgd,rkld->rkgl', queries, cache[..., :HD], preferred_element...  12 us
    dot_general x1, matrix products, attend_full(): jnp.einsum('rkgl,rkld->rkgd', probabilities, cache[..., HD:], preferred_e...  9.91 us
    all_gather x1, blocking collectives, local(): lax.all_gather(normed, 'head', axis=0, tiled=True)  7.94 us
    all_to_all x1, starting transfers between devices, local(): lax.all_to_all(outgoing, 'req', split_axis=0, concat_axis=0, tiled=True)  5.52 us
    dot_general x1, matrix products, local(): jnp.einsum('sjcd,jdf->sjcf', lax.all_to_all(outgoing, 'req', split_axis=0...  5.07 us
  transfers between devices with their start and end apart: 3, of which 3 were waited for; matrix products, arithmetic and copies ran while one was open for 3% of the time, Pallas kernels for 0%

commit v1 on v0

--- a/solution.py
+++ b/solution.py
@@ -10,6 +10,28 @@
 F = 512
 EPSILON = 1e-06
 THETA = 10000.0
+
+
+def in_order(parts, dim):
+    dims = list(parts.shape[1:])
+    dims[dim] *= parts.shape[0]
+    return jnp.moveaxis(parts, 0, dim).reshape(dims)
+
+
+def grow_blocks(x, axis):
+    count = lax.axis_size(axis)
+    blocks = x[None]
+    for level in range(count.bit_length() - 1):
+        bit = 1 << level
+        theirs = lax.ppermute(blocks, axis, [(i, i ^ bit) for i in range(count)])
+        both = jnp.stack([blocks, theirs])
+        upper = lax.axis_index(axis) >> level & 1
+        blocks = jnp.where(upper == 0, both, both[::-1]).reshape(-1, *x.shape)
+    return blocks
+
+
+def collect(shard, axis, dim):
+    return in_order(grow_blocks(shard, axis), dim)
 
 
 def rms_scale(values, gain):
@@ -89,11 +111,7 @@
     kv_local = w_qkv.shape[1]
     normed = rms_scale(residual_in, attn_gain)
     flat_weight = w_qkv.reshape(D, kv_local * (group + 2) * HD)
-    projected = jnp.dot(
-        lax.all_gather(normed, "head", axis=0, tiled=True),
-        flat_weight,
-        preferred_element_type=jnp.float32,
-    )
+    projected = jnp.dot(collect(normed, "head", 0), flat_weight, preferred_element_type=jnp.float32)
     queries, new_keys, new_values = project_heads(projected, lengths, group, HD)
     new_kv = jnp.concatenate([new_keys, new_values], axis=-1)
     heads_out = attend_full(queries, new_keys, new_values, kv_cache, lengths)

time: 165 us -> 166 us (level)
  blocking collectives: 7.94 us -> 0 us
  waiting for transfers between devices: 73.8 us -> 79 us
  starting transfers between devices: 9.81 us -> 13.3 us
    all_gather x1 -> x0, blocking collectives: 7.94 us -> none  [local(): lax.all_gather(normed, 'head', axis=0, tiled=True)]
    ppermute x0 -> x2, waiting for transfers between devices: none -> 4.59 us  [grow_blocks(): theirs = lax.ppermute(blocks, axis, [(i, i ^ bit) for i in range(count)])]
    ppermute x0 -> x2, starting transfers between devices: none -> 3.45 us  [grow_blocks(): theirs = lax.ppermute(blocks, axis, [(i, i ^ bit) for i in range(count)])]
  transfers between devices with their start and end apart: 3 -> 5, of which waited for: 3 -> 5; matrix products, arithmetic and copies ran while one was open for 3% -> 4% of each run, Pallas kernels for 0% -> 0%
where the time goes in v1:
time: 166 us; the launch traced here: 165 us
  waiting for transfers between devices  79 us (48%)
  matrix products  32.6 us (20%)
  local copies, waits for them, and re-layouts  14.4 us (9%)
  between operations  14.4 us (9%)
  starting transfers between devices  13.3 us (8%)
  other arithmetic  11.4 us (7%)
    all_to_all x1, waiting for transfers between devices, local(): lax.all_to_all(outgoing, 'req', split_axis=0, concat_axis=0, tiled=True)  28.4 us
    all_to_all x1, waiting for transfers between devices, local(): lax.all_to_all(result, 'req', split_axis=0, concat_axis=0, tiled=True)  24.7 us
    reduce_scatter x1, waiting for transfers between devices, local(): lax.psum_scatter(jnp.dot(attn_heads, w_out, preferred_element_type=jnp.fl...  21.2 us
    dot_general x1, matrix products, attend_full(): jnp.einsum('rkgd,rkld->rkgl', queries, cache[..., :HD], preferred_element...  12 us
    dot_general x1, matrix products, attend_full(): jnp.einsum('rkgl,rkld->rkgd', probabilities, cache[..., HD:], preferred_e...  9.91 us
    all_to_all x1, starting transfers between devices, local(): lax.all_to_all(outgoing, 'req', split_axis=0, concat_axis=0, tiled=True)  5.52 us
    dot_general x1, matrix products, local(): jnp.einsum('sjcd,jdf->sjcf', lax.all_to_all(outgoing, 'req', split_axis=0...  5.07 us
    ppermute x2, waiting for transfers between devices, grow_blocks(): theirs = lax.ppermute(blocks, axis, [(i, i ^ bit) for i in range(count)])  4.59 us
  transfers between devices with their start and end apart: 5, of which 5 were waited for; matrix products, arithmetic and copies ran while one was open for 4% of the time, Pallas kernels for 0%

profile of v1, /device:TPU:0, one launch (start us, length us, event | category | flops | bytes accessed | tf_op | source)
XLA Modules:
  0.0 165.1 jit_solution(1620900940691937217)
XLA Ops:
  7.2 1.2 fusion.44
  8.4 0.7 convert_element_type.114
  9.1 1.0 fusion.61
  11.6 2.9 %collective-permute-start.1 = (bf16[2,32,1536]{2,1,0:T(8,128)(2,1)S(1)}, bf16[2,32,1536]{2,1,0:T(8,128)(2,1)S(1)}, u32[]{:S(2)}, u32[]{:S(2)}) collective-permute-start(bf16[2,32,1536]{2,1,0:T(8,128)(2,1)S(1)} %get-tuple-element.17), channel_id=1, source_target_pairs={{0,2},{1,3},{2,0},{3,1},{4,6},{5,7},{6,4},{7,5},{8,10},{9,11},{10,... | collective-permute-start | bytes 589832 | tf_op jit(solution)/shard_map/ppermute | solution.py:26
  14.5 0.7 iota_compare_fusion.2
  15.3 4.5 %collective-permute-done.1 = bf16[2,32,1536]{2,1,0:T(8,128)(2,1)S(1)} collective-permute-done((bf16[2,32,1536]{2,1,0:T(8,128)(2,1)S(1)}, bf16[2,32,1536]{2,1,0:T(8,128)(2,1)S(1)}, u32[]{:S(2)}, u32[]{:S(2)}) %collective-permute-start.1) | collective-permute-done | bytes 196640 | tf_op jit(solution)/shard_map/ppermute | solution.py:26
  20.7 0.8 copy.89
  21.7 12.0 %fusion.71 = (f32[128,2,3]{2,1,0:T(2,128)}, f32[128,2,3,192]{3,2,1,0:T(4,128)S(1)}) fusion(bf16[128,2,3,64]{3,2,1,0:T(4,128)(2,1)S(1)} %copy.81, bf16[128,2,192,128]{3,2,1,0:T(8,128)(2,1)} %param.15, pred[128,192]{1,0:T(8,128)(4,1)S(1)} %iota_compare_fusion.2), kind=kOutput, calls=%fused_computation.107 | convolution fusion | flops 19315968 | bytes 13298688 | tf_op jit(solution)/shard_map/rkgd,rkld->rkgl/dot_general | solution.py:76
  33.7 1.1 copy.85
  34.9 0.8 fusion.35
  35.9 0.8 copy.88
  36.7 0.8 copy.91
  37.5 9.9 %fusion.30 = bf16[128,2,3,64]{3,2,1,0:T(4,128)(2,1)} fusion(bf16[128,2,192,128]{3,2,1,0:T(8,128)(2,1)} %param.15, f32[128,2,3,192]{3,2,1,0:T(4,128)} %copy-done.3, f32[128,2,3]{2,1,0:T(2,128)S(1)} %copy.86, pred[128,192]{1,0:T(8,128)(4,1)S(1)} %iota_compare_fusion.2, f32[128,2,3]{2,1,0:T(2,128)} %copy.91, f32[128,2,64]{2,1,0:T(2,128)} %copy.89, ...), kind=kOutput, calls=%fused_computation.22 | convolution fusion | flops 19513344 | bytes 13370368 | tf_op jit(solution)/shard_map/rkgl,rkld->rkgd/dot_general | solution.py:88
  47.4 1.1 copy.92
  48.5 1.1 convolution_convert_fusion.1
  50.9 21.2 %reduce-scatter.2.cloned.1.call-done = bf16[32,1536]{1,0:T(8,128)(2,1)} async-done(((bf16[128,1536]{1,0:T(8,128)(2,1)}), bf16[32,1536]{1,0:T(8,128)(2,1)}) %reduce-scatter.2.cloned.1.call-update) | async-done | bytes 98320 | tf_op jit(solution)/shard_map/reduce_scatter | solution.py:120
  72.2 1.0 fusion.48
  73.2 1.0 fusion.50
  74.7 1.2 reshape.245
  75.9 5.5 %all-to-all-start = ((bf16[8,3,12,1536]{3,2,1,0:T(8,128)(2,1)}), bf16[8,3,12,1536]{3,2,1,0:T(8,128)(2,1)S(1)}, u32[]{:S(2)}, u32[]{:S(2)}) async-start(bf16[8,3,12,1536]{3,2,1,0:T(8,128)(2,1)} %reshape.245), calls=%async_computation.1 | async-start | bytes 2359296 | tf_op jit(solution)/shard_map/all_to_all | solution.py:148
  81.6 28.4 %all-to-all-done = bf16[8,3,12,1536]{3,2,1,0:T(8,128)(2,1)S(1)} async-done(((bf16[8,3,12,1536]{3,2,1,0:T(8,128)(2,1)}), bf16[8,3,12,1536]{3,2,1,0:T(8,128)(2,1)S(1)}, u32[]{:S(2)}, u32[]{:S(2)}) %all-to-all-start) | async-done | bytes 884768 | tf_op jit(solution)/shard_map/all_to_all | solution.py:148
  110.0 5.1 %fusion.14 = f32[8,3,12,1024]{3,2,0,1:T(8,128)S(1)} fusion(bf16[3,1536,1024]{2,1,0:T(8,128)(2,1)} %param.20, bf16[8,3,12,1536]{3,2,1,0:T(8,128)(2,1)S(1)} %all-to-all-done), kind=kOutput, calls=%fused_computation.15 | convolution fusion | flops 905969664 | bytes 11501568 | tf_op jit(solution)/shard_map/sjcd,jdf->sjcf/dot_general | solution.py:146
  115.1 3.2 %fusion.11 = bf16[8,3,12,1536]{3,2,0,1:T(8,128)(2,1)S(1)} fusion(bf16[3,512,1536]{2,1,0:T(8,128)(2,1)} %param.21, f32[8,3,12,1024]{3,2,0,1:T(8,128)S(1)} %fusion.14), kind=kOutput, calls=%fused_computation.12 | convolution fusion | flops 454311936 | bytes 6782976 | tf_op jit(solution)/shard_map/sjcf,jfd->sjcd/dot_general | solution.py:153
  118.3 1.1 copy.101
  119.4 4.2 %all-to-all-start.1 = ((bf16[8,3,12,1536]{3,2,1,0:T(8,128)(2,1)}), bf16[8,3,12,1536]{3,2,1,0:T(8,128)(2,1)}, u32[]{:S(2)}, u32[]{:S(2)}) async-start(bf16[8,3,12,1536]{3,2,1,0:T(8,128)(2,1)} %copy.101), calls=%async_computation.2 | async-start | bytes 2359296 | tf_op jit(solution)/shard_map/all_to_all | solution.py:156
  123.9 0.8 copy.102
  124.8 2.0 %gather_fusion.1 = f32[256]{0:T(256)S(1)} fusion(f32[32,24]{0,1:T(8,128)S(1)} %fusion.73, s32[256]{0:T(256)S(1)} %reshape.255), kind=kCustom, calls=%fused_computation.1 | custom fusion | bytes 4096 | tf_op jit(solution)/shard_map/jit(take_along_axis)/gather | solution.py:129
  127.3 24.7 %all-to-all-done.1 = bf16[8,3,12,1536]{3,2,1,0:T(8,128)(2,1)} async-done(((bf16[8,3,12,1536]{3,2,1,0:T(8,128)(2,1)}), bf16[8,3,12,1536]{3,2,1,0:T(8,128)(2,1)}, u32[]{:S(2)}, u32[]{:S(2)}) %all-to-all-start.1) | async-done | bytes 884768 | tf_op jit(solution)/shard_map/all_to_all | solution.py:156
  152.1 1.3 reshape.246
  153.4 2.1 %gather_fusion = bf16[256,1536]{1,0:T(8,128)(2,1)} fusion(bf16[288,1536]{1,0:T(8,128)(2,1)S(1)} %reshape.246, s32[1024]{0:T(1024)S(1)} %pad_clamp_fusion), kind=kCustom, calls=%fused_computation | custom fusion | bytes 1573888 | tf_op jit(solution)/shard_map/jit(_take)/gather | solution.py:157
  155.5 2.0 %multiply_reduce_fusion = f32[32,1536]{1,0:T(8,128)S(1)} fusion(bf16[256,1536]{1,0:T(8,128)(2,1)} %gather_fusion, f32[32,8]{1,0:T(8,128)S(1)} %fusion.64, pred[32,8]{1,0:T(8,128)(4,1)S(1)} %compare_and_fusion), kind=kLoop, calls=%fused_computation.14 | loop fusion | flops 1523712 | bytes 984320 | tf_op jit(solution)/shard_map/reduce_sum | solution.py:160
  157.5 0.7 fusion.51
  (67 shorter events, 5.6 us)
Async XLA Ops:
  7.2 12.7 %copy-start = (bf16[1536,2,320]{0,2,1:T(8,128)(2,1)S(1)}, bf16[1536,2,320]{0,2,1:T(8,128)(2,1)}, u32[]{:S(2)}) copy-start(bf16[1536,2,320]{0,2,1:T(8,128)(2,1)} %param.13) | copy-start | bytes 5898244
  7.2 65.0 %reduce-scatter.2.cloned.1.call-start = ((), (), s32[]{:S(2)}) async-start(), calls=%async_computation.3 | async-start | bytes 491520 | tf_op jit(solution)/shard_map/reduce_scatter | solution.py:120
  10.1 1.5 collective-permute-start
  11.6 8.2 %collective-permute-start.1 = (bf16[2,32,1536]{2,1,0:T(8,128)(2,1)S(1)}, bf16[2,32,1536]{2,1,0:T(8,128)(2,1)S(1)}, u32[]{:S(2)}, u32[]{:S(2)}) collective-permute-start(bf16[2,32,1536]{2,1,0:T(8,128)(2,1)S(1)} %get-tuple-element.17), channel_id=1, source_target_pairs={{0,2},{1,3},{2,0},{3,1},{4,6},{5,7},{6,4},{7,5},{8,10},{9,11},{10,... | collective-permute-start | bytes 589832 | tf_op jit(solution)/shard_map/ppermute | solution.py:26
  33.6 3.0 %copy-start.3 = (f32[128,2,3,192]{3,2,1,0:T(4,128)}, f32[128,2,3,192]{3,2,1,0:T(4,128)S(1)}, u32[]{:S(2)}) copy-start(f32[128,2,3,192]{3,2,1,0:T(4,128)S(1)} %get-tuple-element.25) | copy-start | bytes 1769476
  37.5 11.1 %copy-start.2 = (bf16[384,1536]{1,0:T(8,128)(2,1)S(1)}, bf16[384,1536]{1,0:T(8,128)(2,1)}, u32[]{:S(2)}) copy-start(bf16[384,1536]{1,0:T(8,128)(2,1)} %param.14) | copy-start | bytes 3538948
  47.4 2.3 %copy-start.6 = (s32[32,8]{0,1:T(8,128)S(1)}, s32[32,8]{0,1:T(8,128)}, u32[]{:S(2)}) copy-start(s32[32,8]{0,1:T(8,128)} %param.19) | copy-start | bytes 3076
  47.4 2.6 %copy-start.7 = (bf16[1536]{0:T(1024)(128)(2,1)S(1)}, bf16[1536]{0:T(1024)(128)(2,1)}, u32[]{:S(2)}) copy-start(bf16[1536]{0:T(1024)(128)(2,1)} %param.17) | copy-start | bytes 9220
  47.4 24.8 %copy-start.1 = (bf16[32,1536]{1,0:T(8,128)(2,1)S(1)}, bf16[32,1536]{1,0:T(8,128)(2,1)}, u32[]{:S(2)}) copy-start(bf16[32,1536]{1,0:T(8,128)(2,1)} %param.11) | copy-start | bytes 294916
  75.9 34.1 %all-to-all-start = ((bf16[8,3,12,1536]{3,2,1,0:T(8,128)(2,1)}), bf16[8,3,12,1536]{3,2,1,0:T(8,128)(2,1)S(1)}, u32[]{:S(2)}, u32[]{:S(2)}) async-start(bf16[8,3,12,1536]{3,2,1,0:T(8,128)(2,1)} %reshape.245), calls=%async_computation.1 | async-start | bytes 2359296 | tf_op jit(solution)/shard_map/all_to_all | solution.py:148
  118.3 6.3 %copy-start.5 = (bf16[1536,24]{0,1:T(8,128)(2,1)S(1)}, bf16[1536,24]{0,1:T(8,128)(2,1)}, u32[]{:S(2)}) copy-start(bf16[1536,24]{0,1:T(8,128)(2,1)} %param.18) | copy-start | bytes 221188
  119.4 32.6 %all-to-all-start.1 = ((bf16[8,3,12,1536]{3,2,1,0:T(8,128)(2,1)}), bf16[8,3,12,1536]{3,2,1,0:T(8,128)(2,1)}, u32[]{:S(2)}, u32[]{:S(2)}) async-start(bf16[8,3,12,1536]{3,2,1,0:T(8,128)(2,1)} %copy.101), calls=%async_computation.2 | async-start | bytes 2359296 | tf_op jit(solution)/shard_map/all_to_all | solution.py:156
  153.4 4.1 %copy-start.4 = (bf16[32,1536]{1,0:T(8,128)(2,1)S(1)}, bf16[32,1536]{1,0:T(8,128)(2,1)}, u32[]{:S(2)}) copy-start(bf16[32,1536]{1,0:T(8,128)(2,1)} %reduce-scatter.2.cloned.1.call-done) | copy-start | bytes 294916
Sparse Core Ops, SparseCore 0:
  49.8 22.2 reduce-scatter.1
